TPU v7x, 32 devices: a whole 2x2x4 slice. The times are simulated.
32 devices in a mesh: dp: 4 (over y, core), seq: 8 (over z, x).
Axes of the slice: x: 2, y: 2, z: 4, core: 2. Of those that a mesh axis runs over, the one named last changes fastest.
Arguments:
- tokens: bfloat16 [4, 24, 256, 1280], P('dp', 'seq'), may hold values from -6 to 6
- clip_ids: int32 [4, 24], P('dp'), may hold values from 0 to 5, never falling along the last dimension, each value on 1 to 12 neighbouring positions
- ln_gain: float32 [1280], replicated, may hold values from 0.1 to 1.9
- w_qkv: bfloat16 [1280, 1920], P(None, 'dp'), may hold values from -0.15625 to 0.15625
- w_out: bfloat16 [640, 1280], P(None, 'dp'), may hold values from -0.25 to 0.25
Outputs:
- output: bfloat16 [4, 24, 256, 1280], P('dp', 'seq')
Inputs may be any that keep to these rules, and one draw needn't show every extreme that they name: `clip_ids`: in each batch the clip numbers never fall along the frames, every clip number occurs, each clip covers 1 to 12 consecutive frames, and some clip covers exactly 12.
All inputs are finite; a program needn't handle non-finite values.
Results may differ from a plain program's by a relative error of at most 0.006.
Values may be sent and summed in bfloat16 or wider, within the bound.
A program may use at most 64 MiB of HBM per device.

v0:
```python
import math
import jax
import jax.numpy as jnp
from jax import lax
from jax.sharding import PartitionSpec as P

HS = 80
HEADS = 8
HD = 640
norm_eps = 1e-05


def layer_norm(block, ln_gain):
    values = block.astype(jnp.float32)
    center = jnp.mean(values, axis=-1, keepdims=True)
    spread = jnp.mean(jnp.square(values - center), axis=-1, keepdims=True)
    return ((values - center) * lax.rsqrt(spread + norm_eps) * ln_gain).astype(jnp.bfloat16)


def split_heads(projected):
    queries = (projected[:, :HD] * (1.0 / math.sqrt(HS))).astype(jnp.bfloat16)
    keys = projected[:, HD : 2 * HD].astype(jnp.bfloat16)
    values = projected[:, 2 * HD :].astype(jnp.bfloat16)
    return (queries, keys, values)


def attend(queries, keys, values, clip_row):
    scores = jnp.einsum("flhe,glhe->lhfg", queries, keys, preferred_element_type=jnp.float32)
    same_clip = clip_row[:, None] == clip_row[None, :]
    raised = jnp.where(same_clip, jnp.exp(scores), jnp.zeros_like(scores))
    attn_probs = (raised / jnp.sum(raised, axis=-1, keepdims=True)).astype(jnp.bfloat16)
    return jnp.einsum(
        "lhfg,glhe->flhe", attn_probs, values, preferred_element_type=jnp.float32
    ).astype(jnp.bfloat16)


def shards(tokens, clip_ids, ln_gain, w_qkv, w_out):
    width = tokens.shape[3]
    clip_row = clip_ids[0]
    frames = clip_row.shape[0]
    local_frames = tokens.shape[1]
    patches = tokens.shape[2]
    moved = lax.all_to_all(tokens, "seq", split_axis=2, concat_axis=1, tiled=True)
    places = moved.shape[2]
    normed = layer_norm(moved, ln_gain).reshape(frames * places, width)

    def column_block(piece, start):
        return jnp.dot(normed, piece, preferred_element_type=jnp.float32)

    queries, keys, values = split_heads(
        column_block(lax.all_gather(w_qkv, "dp", axis=1, tiled=True), jnp.int32(0))
    )
    head_shape = (frames, places, HEADS, HS)
    mixed = attend(
        queries.reshape(head_shape), keys.reshape(head_shape), values.reshape(head_shape), clip_row
    )
    mixed = lax.all_to_all(
        mixed.reshape(1, frames, places, HD), "seq", split_axis=1, concat_axis=2, tiled=True
    )
    row_count = local_frames * patches
    rows_in = mixed.reshape(row_count, HD)

    def column_block(piece, start):
        return jnp.dot(rows_in, piece, preferred_element_type=jnp.float32)

    update = column_block(lax.all_gather(w_out, "dp", axis=1, tiled=True), jnp.int32(0))
    summed = tokens.reshape(row_count, width).astype(jnp.float32) + update
    return summed.astype(jnp.bfloat16).reshape(tokens.shape)


def solution(mesh):
    placed = (P("dp", "seq", None, None), P("dp", None), P(), P(None, "dp"), P(None, "dp"))
    return jax.shard_map(
        shards, mesh=mesh, in_specs=placed, out_specs=P("dp", "seq", None, None), check_vma=False
    )
```

profile of v0, /device:TPU:0, one launch (start us, length us, event | category | flops | bytes accessed | tf_op | source)
XLA Modules:
  0.0 151.9 jit_solution(18149255715372341711)
XLA Ops:
  6.5 0.0 all-gather.3.cloned.1.call-start
  6.5 0.7 all-gather.3.cloned.1.call-update
  7.3 4.8 %copy.35 = bf16[1,3,256,1280]{3,1,0,2:T(4,128)(2,1)} copy(bf16[1,3,256,1280]{3,2,1,0:T(8,128)(2,1)} %param.5) | data formatting | bytes 3932160 | tf_op args[0]
  12.0 0.0 copy-start.2
  12.0 7.4 %all-to-all-start = ((bf16[1,3,256,1280]{3,1,0,2:T(4,128)(2,1)}), bf16[1,3,256,1280]{3,1,0,2:T(4,128)(2,1)S(1)}, u32[]{:S(2)}, u32[]{:S(2)}) async-start(bf16[1,3,256,1280]{3,1,0,2:T(4,128)(2,1)} %copy.35), calls=%async_computation | async-start | bytes 5242880 | tf_op jit(solution)/shard_map/all_to_all | solution.py:43
  19.4 0.0 all-gather.5.cloned.1.call-start
  19.5 0.7 all-gather.5.cloned.1.call-update
  20.2 0.0 copy-done.2
  20.2 0.1 broadcast_compare_fusion
  20.3 58.6 %all-to-all-done = bf16[1,3,256,1280]{3,1,0,2:T(4,128)(2,1)S(1)} async-done(((bf16[1,3,256,1280]{3,1,0,2:T(4,128)(2,1)}), bf16[1,3,256,1280]{3,1,0,2:T(4,128)(2,1)S(1)}, u32[]{:S(2)}, u32[]{:S(2)}) %all-to-all-start) | async-done | bytes 1966112 | tf_op jit(solution)/shard_map/all_to_all | solution.py:43
  78.9 2.3 %convert_bitcast_fusion = (f32[1,8,3,32,1280]{4,3,1,2,0:T(8,128)}, bf16[1,3,256,1280]{3,2,1,0:T(8,128)(2,1)S(1)}) fusion(bf16[1,3,256,1280]{3,1,0,2:T(4,128)(2,1)S(1)} %all-to-all-done), kind=kLoop, calls=%fused_computation.1 | loop fusion | flops 983040 | bytes 7864320 | tf_op jit(solution)/shard_map/convert_element_type | solution.py:14
  81.2 0.3 fusion.5
  81.6 0.7 multiply_reduce_fusion
  82.3 0.1 rsqrt.12
  82.4 0.1 div.17
  82.4 0.0 copy-start.1
  82.4 2.4 %copy.37 = f32[1,8,3,32,1280]{4,3,2,1,0:T(8,128)S(1)} copy(f32[1,8,3,32,1280]{4,3,1,2,0:T(8,128)} %get-tuple-element.5) | data formatting | bytes 7864320 | tf_op jit(solution)/shard_map/convert_element_type | solution.py:14
  84.9 0.0 copy-done.1
  84.9 0.6 fusion.2
  85.4 0.0 all-gather.3.cloned.1.call-done
  85.5 8.5 %fusion.18 = (bf16[768,1920]{1,0:T(8,128)(2,1)S(1)}, f32[768,1920]{1,0:T(8,128)}) fusion(bf16[768,1280]{1,0:T(8,128)(2,1)S(1)} %fusion.2, bf16[1280,1920]{0,1:T(8,128)(2,1)} %all-gather.3.cloned.1.call-done), kind=kOutput, calls=%fused_computation.27 | convolution fusion | flops 3776348160 | bytes 15728640 | tf_op jit(solution)/shard_map/dot_general | solution.py:48
  94.0 0.2 fusion.17
  94.2 1.6 %reshape.90 = bf16[24,32,8,80]{3,2,1,0:T(8,128)(2,1)S(1)} reshape(bf16[768,640]{1,0:T(8,128)(2,1)S(1)} %get-tuple-element.8) | data formatting | bytes 1966080 | tf_op jit(solution)/shard_map/reshape | solution.py:55
  95.8 1.7 %fusion.6 = bf16[768,640]{1,0:T(8,128)(2,1)S(1)} fusion(f32[768,1920]{1,0:T(8,128)} %get-tuple-element.10), kind=kLoop, calls=%fused_computation.13 | loop fusion | flops 983040 | bytes 2949120 | tf_op jit(solution)/shard_map/convert_element_type | solution.py:21
  97.5 2.5 %reshape.89 = bf16[24,32,8,80]{3,2,1,0:T(8,128)(2,1)} reshape(bf16[768,640]{1,0:T(8,128)(2,1)S(1)} %fusion.6) | data formatting | bytes 1966080 | tf_op jit(solution)/shard_map/reshape | solution.py:55
  100.0 5.7 %fusion.4 = (f32[32,8,24]{2,1,0:T(8,128)S(1)}, f32[32,8,24,24]{2,3,1,0:T(8,128)}) fusion(pred[24,24]{0,1:T(8,128)(4,1)S(1)} %broadcast_compare_fusion, bf16[24,32,8,80]{3,2,1,0:T(8,128)(2,1)S(1)} %reshape.90, bf16[24,32,8,80]{3,2,1,0:T(8,128)(2,1)} %reshape.89), kind=kOutput, calls=%fused_computation.10 | convolution fusion | flops 23881728 | bytes 2581056 | tf_op jit(solution)/shard_map/flhe,glhe->lhfg/dot_general | solution.py:28
  105.7 1.6 %reshape.88 = bf16[24,32,8,80]{3,2,1,0:T(8,128)(2,1)S(1)} reshape(bf16[768,640]{1,0:T(8,128)(2,1)S(1)} %get-tuple-element.7) | data formatting | bytes 1966080 | tf_op jit(solution)/shard_map/reshape | solution.py:55
  107.3 3.4 %fusion.13 = bf16[24,32,8,80]{3,0,2,1:T(8,128)(2,1)S(1)} fusion(f32[32,8,24,24]{2,3,1,0:T(8,128)} %get-tuple-element.12, f32[32,8,24]{2,1,0:T(8,128)S(1)} %get-tuple-element.11, pred[24,24]{0,1:T(8,128)(4,1)S(1)} %broadcast_compare_fusion, bf16[24,32,8,80]{3,2,1,0:T(8,128)(2,1)S(1)} %reshape.88), kind=kOutput, calls=%fused_computation.21 | convolution fusion | flops 24526848 | bytes 2581056 | tf_op jit(solution)/shard_map/lhfg,glhe->flhe/dot_general | solution.py:32
  110.7 0.3 copy.44
  111.1 1.2 reshape.91
  112.3 0.0 copy-start
  112.3 28.2 %all_to_all.24 = bf16[1,24,32,640]{3,2,0,1:T(8,128)(2,1)S(1)} all-to-all(bf16[1,24,32,640]{3,2,0,1:T(8,128)(2,1)S(1)} %bitcast.36), channel_id=1, replica_groups=mesh['dp'=4,'seq'=8] {'seq'}, dimensions={1} | all-to-all | bytes 1966080 | tf_op jit(solution)/shard_map/all_to_all | solution.py:57
  140.5 0.1 copy.46
  140.6 0.0 all-gather.5.cloned.1.call-done
  140.6 0.0 copy-done
  140.6 4.4 %fusion.3 = bf16[768,1280]{1,0:T(8,128)(2,1)} fusion(bf16[768,640]{1,0:T(8,128)(2,1)S(1)} %bitcast.39, bf16[640,1280]{0,1:T(8,128)(2,1)} %all-gather.5.cloned.1.call-done, bf16[768,1280]{1,0:T(8,128)(2,1)S(1)} %bitcast.38), kind=kOutput, calls=%fused_computation.7 | convolution fusion | flops 1261240320 | bytes 6553600 | tf_op jit(solution)/shard_map/dot_general | solution.py:64
  (4 shorter events, 0.0 us)
Async XLA Ops:
  6.5 78.9 %all-gather.3.cloned.1.call-start = ((), (), s32[]{:S(2)}) async-start(), calls=%async_computation.2 | async-start | bytes 6144000 | tf_op jit(solution)/shard_map/all_gather | solution.py:51
  12.0 8.2 %copy-start.2 = (s32[1,24]{1,0:T(1,128)S(1)}, s32[1,24]{1,0:T(1,128)}, u32[]{:S(2)}) copy-start(s32[1,24]{1,0:T(1,128)} %param.6) | copy-start | bytes 292
  12.0 66.9 %all-to-all-start = ((bf16[1,3,256,1280]{3,1,0,2:T(4,128)(2,1)}), bf16[1,3,256,1280]{3,1,0,2:T(4,128)(2,1)S(1)}, u32[]{:S(2)}, u32[]{:S(2)}) async-start(bf16[1,3,256,1280]{3,1,0,2:T(4,128)(2,1)} %copy.35), calls=%async_computation | async-start | bytes 5242880 | tf_op jit(solution)/shard_map/all_to_all | solution.py:43
  19.4 121.2 %all-gather.5.cloned.1.call-start = ((), (), s32[]{:S(2)}) async-start(), calls=%async_computation.3 | async-start | bytes 2048000 | tf_op jit(solution)/shard_map/all_gather | solution.py:66
  82.4 2.4 %copy-start.1 = (f32[1280]{0:T(1024)S(1)}, f32[1280]{0:T(1024)}, u32[]{:S(2)}) copy-start(f32[1280]{0:T(1024)} %param.7) | copy-start | bytes 15364
  112.3 28.3 %copy-start = (bf16[1,3,256,1280]{3,2,1,0:T(8,128)(2,1)S(1)}, bf16[1,3,256,1280]{3,2,1,0:T(8,128)(2,1)}, u32[]{:S(2)}) copy-start(bf16[1,3,256,1280]{3,2,1,0:T(8,128)(2,1)} %param.5) | copy-start | bytes 5898244
Sparse Core Ops, SparseCore 0:
  8.9 41.2 all-gather.2
  51.8 19.9 all-gather.4
where the time goes:
time: 152 us
  waiting for transfers between devices  60.1 us (40%)
  blocking collectives  28.2 us (19%)
  matrix products  22 us (14%)
  local copies, waits for them, and re-layouts  14.9 us (10%)
  between operations  13.6 us (9%)
  starting transfers between devices  7.45 us (5%)
  other arithmetic  5.69 us (4%)
    all_to_all x1, waiting for transfers between devices, shards(): lax.all_to_all(tokens, 'seq', split_axis=2, concat_axis=1, tiled=True)  58.6 us
    all_to_all x1, blocking collectives, shards(): lax.all_to_all(mixed.reshape(1, frames, places, HD), 'seq', split_axis=1,...  28.2 us
    dot_general x1, matrix products, column_block(): return jnp.dot(normed, piece, preferred_element_type=jnp.float32)  8.52 us
    all_to_all x1, starting transfers between devices, shards(): lax.all_to_all(tokens, 'seq', split_axis=2, concat_axis=1, tiled=True)  7.41 us
    dot_general x1, matrix products, attend(): jnp.einsum('flhe,glhe->lhfg', queries, keys, preferred_element_type=jnp.f...  5.69 us
    unnamed x7, local copies, waits for them, and re-layouts  4.77 us
    dot_general x1, matrix products, column_block(): return jnp.dot(rows_in, piece, preferred_element_type=jnp.float32)  4.43 us
    dot_general x1, matrix products, attend(): jnp.einsum('lhfg,glhe->flhe', attn_probs, values, preferred_element_type=...  3.4 us
  transfers between devices with their start and end apart: 3, of which 1 were waited for; matrix products, arithmetic and copies ran while one was open for 25% of the time, Pallas kernels for 0%

commit v1 on v0

--- a/solution.py
+++ b/solution.py
@@ -40,7 +40,10 @@
     frames = clip_row.shape[0]
     local_frames = tokens.shape[1]
     patches = tokens.shape[2]
-    moved = lax.all_to_all(tokens, "seq", split_axis=2, concat_axis=1, tiled=True)
+    moved = jnp.concatenate(
+        lax.all_to_all(jnp.stack(jnp.split(tokens, lax.axis_size("seq"), axis=2)), "seq", 0, 0),
+        axis=1,
+    )
     places = moved.shape[2]
     normed = layer_norm(moved, ln_gain).reshape(frames * places, width)
 

time: 152 us -> 140 us (0.921)
  waiting for transfers between devices: 60.1 us -> 46 us
  local copies, waits for them, and re-layouts: 14.9 us -> 16.7 us
    all_to_all x1, waiting for transfers between devices: 58.6 us -> 44.6 us  [shards(): lax.all_to_all(jnp.stack(jnp.split(tokens, lax.axis_size('seq'), axis=2))...]
    unnamed x7 -> x15, local copies, waits for them, and re-layouts: 4.77 us -> 8.28 us
    convert_element_type x1 -> x0, local copies, waits for them, and re-layouts: 2.42 us -> none  [layer_norm(): values = block.astype(jnp.float32)]
    convert_element_type x1 -> x0, other arithmetic: 2.34 us -> none  [layer_norm(): values = block.astype(jnp.float32)]
  transfers between devices with their start and end apart: 3 -> 3, of which waited for: 1 -> 1; matrix products, arithmetic and copies ran while one was open for 25% -> 28% of each run, Pallas kernels for 0% -> 0%
where the time goes in v1:
time: 140 us
  waiting for transfers between devices  46 us (33%)
  blocking collectives  28.1 us (20%)
  matrix products  23.4 us (17%)
  local copies, waits for them, and re-layouts  16.7 us (12%)
  between operations  13.5 us (10%)
  starting transfers between devices  7.45 us (5%)
  other arithmetic  4.74 us (3%)
    all_to_all x1, waiting for transfers between devices, shards(): lax.all_to_all(jnp.stack(jnp.split(tokens, lax.axis_size('seq'), axis=2))...  44.6 us
    all_to_all x1, blocking collectives, shards(): lax.all_to_all(mixed.reshape(1, frames, places, HD), 'seq', split_axis=1,...  28.1 us
    dot_general x1, matrix products, column_block(): return jnp.dot(normed, piece, preferred_element_type=jnp.float32)  9.78 us
    unnamed x15, local copies, waits for them, and re-layouts  8.28 us
    all_to_all x1, starting transfers between devices, shards(): lax.all_to_all(jnp.stack(jnp.split(tokens, lax.axis_size('seq'), axis=2))...  7.41 us
    dot_general x1, matrix products, attend(): jnp.einsum('flhe,glhe->lhfg', queries, keys, preferred_element_type=jnp.f...  5.73 us
    dot_general x1, matrix products, column_block(): return jnp.dot(rows_in, piece, preferred_element_type=jnp.float32)  4.42 us
    dot_general x1, matrix products, attend(): jnp.einsum('lhfg,glhe->flhe', attn_probs, values, preferred_element_type=...  3.49 us
  transfers between devices with their start and end apart: 3, of which 1 were waited for; matrix products, arithmetic and copies ran while one was open for 28% of the time, Pallas kernels for 0%

profile of v1, /device:TPU:0, one launch (start us, length us, event | category | flops | bytes accessed | tf_op | source)
XLA Modules:
  0.0 139.9 jit_solution(13695072113758830949)
XLA Ops:
  6.5 0.0 copy-start
  6.5 0.0 all-gather.3.cloned.1.call-start
  6.5 0.7 all-gather.3.cloned.1.call-update
  7.3 1.7 %bitcast_dynamic-update-slice_fusion.7 = bf16[8,1,3,32,1280]{4,3,2,1,0:T(8,128)(2,1)} fusion(bf16[1,3,256,1280]{3,2,1,0:T(8,128)(2,1)} %param.5), kind=kLoop, calls=%fused_computation.28 | loop fusion | bytes 491520
  8.9 1.7 %bitcast_dynamic-update-slice_fusion.6 = bf16[8,1,3,32,1280]{4,3,2,1,0:T(8,128)(2,1)} fusion(bf16[8,1,3,32,1280]{4,3,2,1,0:T(8,128)(2,1)} %bitcast_dynamic-update-slice_fusion.7, bf16[1,3,256,1280]{3,2,1,0:T(8,128)(2,1)} %param.5), kind=kLoop, calls=%fused_computation.27 | loop fusion | bytes 491520
  10.6 0.0 copy-done
  10.6 0.7 bitcast_dynamic-update-slice_fusion.5
  11.3 0.7 bitcast_dynamic-update-slice_fusion.4
  12.0 0.7 bitcast_dynamic-update-slice_fusion.3
  12.7 0.7 bitcast_dynamic-update-slice_fusion.2
  13.4 0.7 bitcast_dynamic-update-slice_fusion.1
  14.1 0.7 bitcast_dynamic-update-slice_fusion
  14.8 0.0 copy-start.3
  14.8 7.4 %all-to-all-start = ((bf16[8,1,3,32,1280]{4,3,2,1,0:T(8,128)(2,1)}), bf16[8,1,3,32,1280]{4,3,2,1,0:T(8,128)(2,1)S(1)}, u32[]{:S(2)}, u32[]{:S(2)}) async-start(bf16[8,1,3,32,1280]{4,3,2,1,0:T(8,128)(2,1)} %bitcast_dynamic-update-slice_fusion), calls=%async_computation | async-start | bytes 3932160 | tf_op jit(solution)/shard_map/all_to_all | solution.py:44
  22.3 0.0 all-gather.5.cloned.1.call-start
  22.3 0.7 all-gather.5.cloned.1.call-update
  23.0 0.0 copy-done.3
  23.0 0.1 broadcast_compare_fusion
  23.1 0.0 copy-start.2
  23.1 44.6 %all-to-all-done = bf16[8,1,3,32,1280]{4,3,2,1,0:T(8,128)(2,1)S(1)} async-done(((bf16[8,1,3,32,1280]{4,3,2,1,0:T(8,128)(2,1)}), bf16[8,1,3,32,1280]{4,3,2,1,0:T(8,128)(2,1)S(1)}, u32[]{:S(2)}, u32[]{:S(2)}) %all-to-all-start) | async-done | bytes 1966112 | tf_op jit(solution)/shard_map/all_to_all | solution.py:44
  67.7 0.3 convert_reduce_fusion
  68.0 0.1 div.17
  68.1 0.7 multiply_reduce_fusion
  68.8 0.1 rsqrt.12
  68.9 0.0 copy-done.2
  68.9 1.9 %fusion.2 = bf16[768,1280]{1,0:T(8,128)(2,1)} fusion(bf16[8,1,3,32,1280]{4,3,2,1,0:T(8,128)(2,1)S(1)} %all-to-all-done, f32[1280]{0:T(1024)S(1)} %copy-done.2, f32[768]{0:T(1024)S(1)} %rsqrt.12, f32[768]{0:T(1024)S(1)} %div.17), kind=kLoop, calls=%fused_computation.4 | loop fusion | flops 4915200 | bytes 3943424 | tf_op jit(solution)/shard_map/convert_element_type | solution.py:17
  70.8 0.0 all-gather.3.cloned.1.call-done
  70.8 9.8 %fusion.17 = (bf16[768,1920]{1,0:T(8,128)(2,1)S(1)}, f32[768,1920]{1,0:T(8,128)}) fusion(bf16[768,1280]{1,0:T(8,128)(2,1)} %fusion.2, bf16[1280,1920]{0,1:T(8,128)(2,1)} %all-gather.3.cloned.1.call-done), kind=kOutput, calls=%fused_computation.34 | convolution fusion | flops 3776348160 | bytes 15728640 | tf_op jit(solution)/shard_map/dot_general | solution.py:51
  80.6 0.2 fusion.16
  80.8 1.6 %reshape.89 = bf16[24,32,8,80]{3,2,1,0:T(8,128)(2,1)S(1)} reshape(bf16[768,640]{1,0:T(8,128)(2,1)S(1)} %get-tuple-element.6) | data formatting | bytes 1966080 | tf_op jit(solution)/shard_map/reshape | solution.py:58
  82.4 1.7 %fusion.5 = bf16[768,640]{1,0:T(8,128)(2,1)S(1)} fusion(f32[768,1920]{1,0:T(8,128)} %get-tuple-element.8), kind=kLoop, calls=%fused_computation.11 | loop fusion | flops 983040 | bytes 2949120 | tf_op jit(solution)/shard_map/convert_element_type | solution.py:21
  84.1 2.5 %reshape.88 = bf16[24,32,8,80]{3,2,1,0:T(8,128)(2,1)} reshape(bf16[768,640]{1,0:T(8,128)(2,1)S(1)} %fusion.5) | data formatting | bytes 1966080 | tf_op jit(solution)/shard_map/reshape | solution.py:58
  86.6 5.7 %fusion.4 = (f32[32,8,24]{2,1,0:T(8,128)S(1)}, f32[32,8,24,24]{2,3,1,0:T(8,128)}) fusion(pred[24,24]{0,1:T(8,128)(4,1)S(1)} %broadcast_compare_fusion, bf16[24,32,8,80]{3,2,1,0:T(8,128)(2,1)S(1)} %reshape.89, bf16[24,32,8,80]{3,2,1,0:T(8,128)(2,1)} %reshape.88), kind=kOutput, calls=%fused_computation.9 | convolution fusion | flops 23881728 | bytes 2581056 | tf_op jit(solution)/shard_map/flhe,glhe->lhfg/dot_general | solution.py:28
  92.3 1.6 %reshape.87 = bf16[24,32,8,80]{3,2,1,0:T(8,128)(2,1)S(1)} reshape(bf16[768,640]{1,0:T(8,128)(2,1)S(1)} %get-tuple-element.5) | data formatting | bytes 1966080 | tf_op jit(solution)/shard_map/reshape | solution.py:58
  94.0 3.5 %fusion.12 = bf16[24,32,8,80]{3,0,2,1:T(8,128)(2,1)S(1)} fusion(f32[32,8,24,24]{2,3,1,0:T(8,128)} %get-tuple-element.10, f32[32,8,24]{2,1,0:T(8,128)S(1)} %get-tuple-element.9, pred[24,24]{0,1:T(8,128)(4,1)S(1)} %broadcast_compare_fusion, bf16[24,32,8,80]{3,2,1,0:T(8,128)(2,1)S(1)} %reshape.87), kind=kOutput, calls=%fused_computation.20 | convolution fusion | flops 24526848 | bytes 2581056 | tf_op jit(solution)/shard_map/lhfg,glhe->flhe/dot_general | solution.py:32
  97.5 0.3 copy.26
  97.8 1.2 reshape.90
  99.0 28.1 %all_to_all.20 = bf16[1,24,32,640]{3,2,0,1:T(8,128)(2,1)S(1)} all-to-all(bf16[1,24,32,640]{3,2,0,1:T(8,128)(2,1)S(1)} %bitcast.41), channel_id=1, replica_groups=mesh['dp'=4,'seq'=8] {'seq'}, dimensions={1} | all-to-all | bytes 1966080 | tf_op jit(solution)/shard_map/all_to_all | solution.py:60
  127.1 0.0 copy-start.1
  127.1 0.1 copy.28
  127.2 0.0 all-gather.5.cloned.1.call-done
  127.2 1.4 %copy-done.1 = bf16[1,3,256,1280]{3,2,1,0:T(8,128)(2,1)S(1)} copy-done((bf16[1,3,256,1280]{3,2,1,0:T(8,128)(2,1)S(1)}, bf16[1,3,256,1280]{3,2,1,0:T(8,128)(2,1)}, u32[]{:S(2)}) %copy-start.1) | copy-done | bytes 1966104
  128.6 4.4 %fusion.3 = bf16[768,1280]{1,0:T(8,128)(2,1)} fusion(bf16[768,640]{1,0:T(8,128)(2,1)S(1)} %bitcast.44, bf16[640,1280]{0,1:T(8,128)(2,1)} %all-gather.5.cloned.1.call-done, bf16[768,1280]{1,0:T(8,128)(2,1)S(1)} %bitcast.43), kind=kOutput, calls=%fused_computation.6 | convolution fusion | flops 1261240320 | bytes 6553600 | tf_op jit(solution)/shard_map/dot_general | solution.py:67
  (2 shorter events, 0.0 us)
Async XLA Ops:
  6.5 4.0 %copy-start = (bf16[1,3,256,1280]{3,2,1,0:T(8,128)(2,1)S(1)}, bf16[1,3,256,1280]{3,2,1,0:T(8,128)(2,1)}, u32[]{:S(2)}) copy-start(bf16[1,3,256,1280]{3,2,1,0:T(8,128)(2,1)} %param.5) | copy-start | bytes 5898244
  6.5 64.3 %all-gather.3.cloned.1.call-start = ((), (), s32[]{:S(2)}) async-start(), calls=%async_computation.2 | async-start | bytes 6144000 | tf_op jit(solution)/shard_map/all_gather | solution.py:54
  14.8 8.2 %copy-start.3 = (s32[1,24]{1,0:T(1,128)S(1)}, s32[1,24]{1,0:T(1,128)}, u32[]{:S(2)}) copy-start(s32[1,24]{1,0:T(1,128)} %param.6) | copy-start | bytes 292
  14.8 52.8 %all-to-all-start = ((bf16[8,1,3,32,1280]{4,3,2,1,0:T(8,128)(2,1)}), bf16[8,1,3,32,1280]{4,3,2,1,0:T(8,128)(2,1)S(1)}, u32[]{:S(2)}, u32[]{:S(2)}) async-start(bf16[8,1,3,32,1280]{4,3,2,1,0:T(8,128)(2,1)} %bitcast_dynamic-update-slice_fusion), calls=%async_computation | async-start | bytes 3932160 | tf_op jit(solution)/shard_map/all_to_all | solution.py:44
  22.3 105.0 %all-gather.5.cloned.1.call-start = ((), (), s32[]{:S(2)}) async-start(), calls=%async_computation.3 | async-start | bytes 2048000 | tf_op jit(solution)/shard_map/all_gather | solution.py:69
  23.1 45.8 %copy-start.2 = (f32[1280]{0:T(1024)S(1)}, f32[1280]{0:T(1024)}, u32[]{:S(2)}) copy-start(f32[1280]{0:T(1024)} %param.7) | copy-start | bytes 15364
  127.1 1.5 %copy-start.1 = (bf16[1,3,256,1280]{3,2,1,0:T(8,128)(2,1)S(1)}, bf16[1,3,256,1280]{3,2,1,0:T(8,128)(2,1)}, u32[]{:S(2)}) copy-start(bf16[1,3,256,1280]{3,2,1,0:T(8,128)(2,1)} %param.5) | copy-start | bytes 5898244
Sparse Core Ops, SparseCore 0:
  8.9 41.2 all-gather.2
  51.8 19.9 all-gather.4
